TPU v7x, 128 devices: a whole 4x4x4 slice. The times are simulated.
128 devices in a mesh: cluster: 8 (over x, core), row: 16 (over z, y).
Axes of the slice: x: 4, y: 4, z: 4, core: 2. Of those that a mesh axis runs over, the one named last changes fastest.
Arguments:
- sources: bfloat16 [32768, 512], P(('cluster', 'row')), may hold values from -12 to 12
- targets: bfloat16 [32768, 512], P(('cluster', 'row')), may hold values from -12 to 12
- source_order: int32 [32768], P(('cluster', 'row')), may hold values from 0 to 255, as said below
- target_order: int32 [32768], P(('cluster', 'row')), may hold values from 0 to 255, as said below
Outputs:
- source_map: bfloat16 [32768, 512], P(('cluster', 'row'))
- target_map: bfloat16 [32768, 512], P(('cluster', 'row'))
Inputs may be any that keep to these rules, and one draw needn't show every extreme that they name: `source_order`: in each aligned block of 256 consecutive rows every value appears exactly once, so each block holds 32 source rows of every co-cluster. `target_order`: in each aligned block of 256 consecutive rows every value appears exactly once, so each block holds 32 target rows of every co-cluster.
All inputs are finite; a program needn't handle non-finite values.
Results may differ from a plain program's by a relative error of at most 0.01.
Values may be sent and summed in bfloat16 or wider, within the bound.
No kernel may reach another device: no remote copies, remote signals or barrier semaphores. Data moves between devices by JAX's collectives and lax.ppermute only.
A program may use at most 64 MiB of HBM per device.

v0:
```python
import math
import jax
import jax.numpy as jnp
from jax import lax
from jax.sharding import PartitionSpec as P

ITERS = 3
entropy_weight = 0.02


def square_sums(matrix):
    widened = matrix.astype(jnp.float32)
    return jnp.sum(widened * widened, axis=1)


def cost_panel(source_rows, source_norms, target_rows, target_norms):
    inner = jnp.einsum("id,jd->ij", source_rows, target_rows, preferred_element_type=jnp.float32)
    return (source_norms[:, None] + target_norms[None, :] - 2.0 * inner) / source_rows.shape[1]


def into_slots(ordering, matrix):
    positions = jnp.arange(matrix.shape[0], dtype=jnp.int32)
    selector = (positions[:, None] == ordering[None, :]).astype(jnp.bfloat16)
    return jnp.dot(selector, matrix, preferred_element_type=jnp.float32).astype(jnp.bfloat16)


def out_of_slots(ordering, matrix):
    positions = jnp.arange(matrix.shape[0], dtype=jnp.int32)
    selector = (ordering[:, None] == positions[None, :]).astype(jnp.bfloat16)
    return jnp.dot(selector, matrix, preferred_element_type=jnp.float32).astype(jnp.bfloat16)


def shards(sources, targets, source_order, target_order):
    rows_dev = sources.shape[0]
    width = sources.shape[1]
    sent_sources = into_slots(source_order, sources)
    sent_targets = into_slots(target_order, targets)
    local_sources, local_targets = (
        lax.all_to_all(sent_sources, "cluster", split_axis=0, concat_axis=0, tiled=True),
        lax.all_to_all(sent_targets, "cluster", split_axis=0, concat_axis=0, tiled=True),
    )
    cluster_targets = lax.all_gather(local_targets, "row", axis=0, tiled=True)
    columns = cluster_targets.shape[0]
    span = 512
    pieces = columns // span
    target_norms = square_sums(cluster_targets)
    target_blocks = cluster_targets.reshape(pieces, span, width)
    norm_blocks = target_norms.reshape(pieces, span)
    source_norms = square_sums(local_sources)
    log_mass = -math.log(columns)

    def row_lse(potential):

        def row_advance(carry, item):
            running, totals = carry
            block, block_norms, block_potential = item
            scores = (
                block_potential[None, :]
                - cost_panel(local_sources, source_norms, block, block_norms)
            ) / entropy_weight
            highest = jnp.maximum(running, jnp.max(scores, axis=1))
            totals = totals * jnp.exp(running - highest) + jnp.sum(
                jnp.exp(scores - highest[:, None]), axis=1
            )
            return ((highest, totals), None)

        start = (jnp.full((rows_dev,), -jnp.inf, jnp.float32), jnp.zeros((rows_dev,), jnp.float32))
        (running, totals), unused = lax.scan(
            row_advance, start, (target_blocks, norm_blocks, potential.reshape(pieces, span))
        )
        return running + jnp.log(totals)

    def column_lse(source_potential):

        def column_advance(carry, item):
            block, block_norms = item
            scores = (
                source_potential[:, None]
                - cost_panel(local_sources, source_norms, block, block_norms)
            ) / entropy_weight
            highest = jnp.max(scores, axis=0)
            return (carry, (highest, jnp.sum(jnp.exp(scores - highest[None, :]), axis=0)))

        unused, (peaks, totals) = lax.scan(column_advance, 0, (target_blocks, norm_blocks))
        peaks = peaks.reshape(-1)
        totals = totals.reshape(-1)
        highest = lax.pmax(peaks, "row")
        summed = lax.psum(totals * jnp.exp(peaks - highest), "row")
        return highest + jnp.log(summed)

    target_potential = jnp.zeros((columns,), jnp.float32)
    for repeat in range(ITERS):
        source_potential = entropy_weight * (log_mass - row_lse(target_potential))
        column_norm = column_lse(source_potential)
        target_potential = entropy_weight * (log_mass - column_norm)
    block = cluster_targets
    block_norms = target_norms
    scores = (
        source_potential[:, None] - cost_panel(local_sources, source_norms, block, block_norms)
    ) / entropy_weight
    weights = jnp.exp(scores - column_norm[None, :]).astype(jnp.bfloat16)
    target_map = lax.psum_scatter(
        jnp.einsum("ij,id->jd", weights, local_sources, preferred_element_type=jnp.float32).astype(
            jnp.bfloat16
        ),
        "row",
        scatter_dimension=0,
        tiled=True,
    )
    row_norm = row_lse(target_potential)

    def accumulate(carry, item):
        block, block_norms, block_potential = item
        scores = (
            block_potential[None, :] - cost_panel(local_sources, source_norms, block, block_norms)
        ) / entropy_weight
        weights = jnp.exp(scores - row_norm[:, None]).astype(jnp.bfloat16)
        return (carry + jnp.dot(weights, block, preferred_element_type=jnp.float32), None)

    source_sums, unused = lax.scan(
        accumulate,
        jnp.zeros((rows_dev, width), jnp.float32),
        (target_blocks, norm_blocks, target_potential.reshape(pieces, span)),
    )
    source_map = source_sums.astype(jnp.bfloat16)
    back_sources, back_targets = (
        lax.all_to_all(source_map, "cluster", split_axis=0, concat_axis=0, tiled=True),
        lax.all_to_all(target_map, "cluster", split_axis=0, concat_axis=0, tiled=True),
    )
    return (out_of_slots(source_order, back_sources), out_of_slots(target_order, back_targets))


def solution(mesh):
    return jax.shard_map(
        shards,
        mesh=mesh,
        in_specs=(
            P(("cluster", "row"), None),
            P(("cluster", "row"), None),
            P(("cluster", "row")),
            P(("cluster", "row")),
        ),
        out_specs=(P(("cluster", "row"), None), P(("cluster", "row"), None)),
        check_vma=False,
    )
```

profile of v0, /device:TPU:1, one launch (start us, length us, event | category | flops | bytes accessed | tf_op | source)
XLA Modules:
  0.0 678.2 jit_solution(1268138748987792291)
XLA Ops:
  9.0 12.2 %all_to_all.48 = bf16[8,32,512]{2,1,0:T(8,128)(2,1)} all-to-all(bf16[8,32,512]{2,1,0:T(8,128)(2,1)S(1)} %bitcast.260), channel_id=1, replica_groups=mesh['cluster'=8,'row'=16] {'cluster'}, dimensions={0} | all-to-all | bytes 524288 | tf_op jit(solution)/shard_map/all_to_all | solution.py:40
  21.2 1.9 convolution_convert_fusion.4
  23.1 4.4 all-to-all-start
  27.6 6.4 all-to-all-done
  34.2 39.4 %all-gather.2.cloned.1.call-done = bf16[4096,512]{1,0:T(8,128)(2,1)} async-done(((bf16[256,512]{1,0:T(8,128)(2,1)}), bf16[4096,512]{1,0:T(8,128)(2,1)}) %all-gather.2.cloned.1.call-update) | async-done | bytes 4194320 | tf_op jit(solution)/shard_map/all_gather | solution.py:42
  73.6 3.1 multiply_reduce_fusion
  76.7 12.7 %while.102 = (s32[]{:T(128)}, f32[256]{0:T(256)S(1)}, f32[256]{0:T(256)S(1)}, f32[256]{0:T(256)S(1)}, f32[8,512]{1,0:T(8,128)S(1)}, /*index=5*/bf16[8,512,512]{2...) while((s32[]{:T(128)}, f32[256]{0:T(256)S(1)}, f32[256]{0:T(256)S(1)}, ...), condition=%wide.region_5.6_spmd.clone, body=%wide.region_2.5_spmd.clone.sunk | while | flops 135398656 | bytes 1856108 | solution.py:68
  89.5 13.7 %while.99 = (s32[]{:T(128)}, f32[8,512]{1,0:T(8,128)S(1)}, f32[8,512]{1,0:T(8,128)S(1)}, f32[256]{0:T(256)S(1)}, f32[256]{0:T(256)S(1)}, /*index=5*/f32[8,512]{1...) while((s32[]{:T(128)}, f32[8,512]{1,0:T(8,128)S(1)}, ...), condition=%wide.region_9.10_spmd, body=%wide.region_6.9_spmd.sunk | while | flops 135396352 | bytes 1858161 | solution.py:84
  89.5 1.4 fusion.151
  91.2 1.4 fusion.151
  92.9 1.4 fusion.151
  94.6 1.4 fusion.151
  96.4 1.4 fusion.151
  98.1 1.4 fusion.151
  99.8 1.4 fusion.151
  101.5 1.4 fusion.151
  103.2 58.3 %pmax.21 = f32[4096]{0:T(1024)S(1)} all-reduce(f32[4096]{0:T(1024)S(1)} %bitcast.268), channel_id=1, replica_groups=mesh['cluster'=8,'row'=16] {'row'}, use_global_device_ids=true, to_apply=%region_10.11 | all-reduce | flops 4096 | bytes 32768 | tf_op jit(solution)/shard_map/pmax | solution.py:87
  161.5 55.6 %psum.21 = f32[4096]{0:T(1024)S(1)} all-reduce(f32[4096]{0:T(1024)S(1)} %exponential_multiply_fusion.2), channel_id=1, replica_groups=mesh['cluster'=8,'row'=16] {'row'}, use_global_device_ids=true, to_apply=%region_11.12 | all-reduce | flops 4096 | bytes 32768 | tf_op jit(solution)/shard_map/psum | solution.py:88
  217.1 12.8 %while.103 = (s32[]{:T(128)}, f32[256]{0:T(256)S(1)}, f32[256]{0:T(256)S(1)}, f32[8,512]{1,0:T(8,128)S(1)}, f32[256]{0:T(256)S(1)}, /*index=5*/f32[8,512]{1,0:T(...) while((s32[]{:T(128)}, f32[256]{0:T(256)S(1)}, ...), condition=%wide.region_15.16_spmd.clone, body=%wide.region_12.15_spmd.clone.sunk | while | flops 135398656 | bytes 1862260 | solution.py:68
  217.2 1.4 fusion.161
  218.8 1.4 fusion.161
  223.6 1.4 fusion.161
  228.4 1.4 fusion.161
  230.0 13.7 %while.100 = (s32[]{:T(128)}, f32[8,512]{1,0:T(8,128)S(1)}, f32[8,512]{1,0:T(8,128)S(1)}, f32[256]{0:T(256)S(1)}, f32[256]{0:T(256)S(1)}, /*index=5*/f32[8,512]{...) while((s32[]{:T(128)}, f32[8,512]{1,0:T(8,128)S(1)}, ...), condition=%wide.region_19.20_spmd, body=%wide.region_16.19_spmd.sunk | while | flops 135396352 | bytes 1858161 | solution.py:84
  230.0 1.4 fusion.153
  231.7 1.4 fusion.153
  233.5 1.4 fusion.153
  235.2 1.4 fusion.153
  236.9 1.4 fusion.153
  238.6 1.4 fusion.153
  240.3 1.4 fusion.153
  242.0 1.4 fusion.153
  243.7 55.6 %pmax.22 = f32[4096]{0:T(1024)S(1)} all-reduce(f32[4096]{0:T(1024)S(1)} %bitcast.270), channel_id=1, replica_groups=mesh['cluster'=8,'row'=16] {'row'}, use_global_device_ids=true, to_apply=%region_20.21 | all-reduce | flops 4096 | bytes 32768 | tf_op jit(solution)/shard_map/pmax | solution.py:87
  299.4 56.0 %psum.22 = f32[4096]{0:T(1024)S(1)} all-reduce(f32[4096]{0:T(1024)S(1)} %exponential_multiply_fusion.1), channel_id=1, replica_groups=mesh['cluster'=8,'row'=16] {'row'}, use_global_device_ids=true, to_apply=%region_21.22 | all-reduce | flops 4096 | bytes 32768 | tf_op jit(solution)/shard_map/psum | solution.py:88
  355.3 12.8 %while.104 = (s32[]{:T(128)}, f32[256]{0:T(256)S(1)}, f32[256]{0:T(256)S(1)}, f32[8,512]{1,0:T(8,128)S(1)}, f32[256]{0:T(256)S(1)}, /*index=5*/f32[8,512]{1,0:T(...) while((s32[]{:T(128)}, f32[256]{0:T(256)S(1)}, ...), condition=%wide.region_25.26_spmd.clone, body=%wide.region_22.25_spmd.clone.sunk | while | flops 135398656 | bytes 1862260 | solution.py:68
  361.8 1.4 fusion.165
  368.2 13.7 %while.101 = (s32[]{:T(128)}, f32[8,512]{1,0:T(8,128)S(1)}, f32[8,512]{1,0:T(8,128)S(1)}, f32[256]{0:T(256)S(1)}, f32[256]{0:T(256)S(1)}, /*index=5*/f32[8,512]{...) while((s32[]{:T(128)}, f32[8,512]{1,0:T(8,128)S(1)}, ...), condition=%wide.region_29.30_spmd, body=%wide.region_26.29_spmd.sunk | while | flops 135396352 | bytes 1858161 | solution.py:84
  368.2 1.4 fusion.155
  369.9 1.4 fusion.155
  371.7 1.4 fusion.155
  373.4 1.4 fusion.155
  375.1 1.4 fusion.155
  376.8 1.4 fusion.155
  378.5 1.4 fusion.155
  380.3 1.4 fusion.155
  382.0 55.6 %pmax.23 = f32[4096]{0:T(1024)S(1)} all-reduce(f32[4096]{0:T(1024)S(1)} %bitcast.272), channel_id=1, replica_groups=mesh['cluster'=8,'row'=16] {'row'}, use_global_device_ids=true, to_apply=%region_30.31 | all-reduce | flops 4096 | bytes 32768 | tf_op jit(solution)/shard_map/pmax | solution.py:87
  437.6 55.6 %psum.23 = f32[4096]{0:T(1024)S(1)} all-reduce(f32[4096]{0:T(1024)S(1)} %exponential_multiply_fusion), channel_id=1, replica_groups=mesh['cluster'=8,'row'=16] {'row'}, use_global_device_ids=true, to_apply=%region_31.32 | all-reduce | flops 4096 | bytes 32768 | tf_op jit(solution)/shard_map/psum | solution.py:88
  493.2 7.0 %convolution_convert_fusion = bf16[4096,512]{1,0:T(8,128)(2,1)} fusion(bf16[256,512]{1,0:T(8,128)(2,1)S(1)} %get-tuple-element.1322, bf16[4096,512]{1,0:T(8,128)(2,1)} %bitcast.254, f32[4096]{0:T(1024)S(1)} %get-tuple-element.614, f32[4096]{0:T(1024)S(1)} %multiply_reduce_fusion, f32[256]{0:T(256)S(1)} %get-tuple-element.1343, f32[256]{0:T(256)S(1)} %get-tuple-element.1345), kind=kOutput, calls=%fused_computation.123 | convolution fusion | flops 2157969408 | bytes 8685568 | tf_op jit(solution)/shard_map/ij,id->jd/dot_general | solution.py:103
  500.2 12.8 %while.105 = (s32[]{:T(128)}, f32[256]{0:T(256)S(1)}, f32[256]{0:T(256)S(1)}, f32[8,512]{1,0:T(8,128)S(1)}, f32[256]{0:T(256)S(1)}, /*index=5*/f32[8,512]{1,0:T(...) while((s32[]{:T(128)}, f32[256]{0:T(256)S(1)}, ...), condition=%wide.region_35.36_spmd.clone, body=%wide.region_32.35_spmd.clone.sunk | while | flops 135398656 | bytes 1862260 | solution.py:68
  503.5 1.4 fusion.169
  508.3 1.4 fusion.169
  513.1 15.4 %while.106 = (s32[]{:T(128)}, f32[256,512]{1,0:T(8,128)S(1)}, f32[8,512]{1,0:T(8,128)S(1)}, f32[256]{0:T(256)S(1)}, f32[8,512]{1,0:T(8,128)S(1)}, /*index=5*/bf1...) while((s32[]{:T(128)}, f32[256,512]{1,0:T(8,128)S(1)}, ...), condition=%wide.region_37.38_spmd.clone, body=%wide.region_36.37_spmd.clone.sunk | while | flops 269746176 | bytes 2374771 | solution.py:120
  513.1 1.9 convolution_add_fusion.2
  515.1 1.9 convolution_add_fusion.2
  517.0 1.9 convolution_add_fusion.2
  518.9 1.9 convolution_add_fusion.2
  520.8 1.9 convolution_add_fusion.2
  522.7 1.9 convolution_add_fusion.2
  524.7 1.9 convolution_add_fusion.2
  526.6 1.9 convolution_add_fusion.2
  528.5 94.9 %all_to_all.49 = bf16[8,32,512]{2,1,0:T(8,128)(2,1)S(1)} all-to-all(bf16[8,32,512]{2,1,0:T(8,128)(2,1)S(1)} %bitcast.255), channel_id=1, replica_groups=mesh['cluster'=8,'row'=16] {'cluster'}, dimensions={0} | all-to-all | bytes 524288 | tf_op jit(solution)/shard_map/all_to_all | solution.py:127
  623.4 33.8 %reduce-scatter.2.cloned.1.call-done = bf16[256,512]{1,0:T(8,128)(2,1)} async-done(((bf16[4096,512]{1,0:T(8,128)(2,1)}), bf16[256,512]{1,0:T(8,128)(2,1)}) %reduce-scatter.2.cloned.1.call-update) | async-done | bytes 262160 | tf_op jit(solution)/shard_map/reduce_scatter | solution.py:102
  657.2 6.7 all-to-all-start.3
  664.9 5.5 all-to-all-done.3
  (340 shorter events, 50.0 us)
Async XLA Ops:
  7.2 1.0 copy-start
  7.2 66.4 %all-gather.2.cloned.1.call-start = ((), (), s32[]{:S(2)}) async-start(), calls=%async_computation.5 | async-start | bytes 4456448 | tf_op jit(solution)/shard_map/all_gather | solution.py:42
  23.1 10.8 %all-to-all-start = ((bf16[8,32,512]{2,1,0:T(8,128)(2,1)}), bf16[8,32,512]{2,1,0:T(8,128)(2,1)S(1)}, u32[]{:S(2)}, u32[]{:S(2)}) async-start(bf16[8,32,512]{2,1,0:T(8,128)(2,1)} %bitcast.15), calls=%async_computation | async-start | bytes 524288 | tf_op jit(solution)/shard_map/all_to_all | solution.py:39
  27.5 629.7 %reduce-scatter.2.cloned.1.call-start = ((), (), s32[]{:S(2)}) async-start(), calls=%async_computation.6 | async-start | bytes 4456448 | tf_op jit(solution)/shard_map/reduce_scatter | solution.py:102
  513.1 150.8 %copy-start.1 = (s32[256]{0:T(256)S(1)}, s32[256]{0:T(256)}, u32[]{:S(2)}) copy-start(s32[256]{0:T(256)} %param.22) | copy-start | bytes 3076
  513.1 157.3 %copy-start.2 = (s32[256]{0:T(256)S(1)}, s32[256]{0:T(256)}, u32[]{:S(2)}) copy-start(s32[256]{0:T(256)} %param.23) | copy-start | bytes 3076
  657.2 13.2 %all-to-all-start.3 = ((bf16[8,32,512]{2,1,0:T(8,128)(2,1)}), bf16[8,32,512]{2,1,0:T(8,128)(2,1)S(1)}, u32[]{:S(2)}, u32[]{:S(2)}) async-start(bf16[8,32,512]{2,1,0:T(8,128)(2,1)} %bitcast.261), calls=%async_computation.4 | async-start | bytes 524288 | tf_op jit(solution)/shard_map/all_to_all | solution.py:128
Sparse Core Ops, SparseCore 0:
  21.3 52.2 all-gather.1
  500.3 156.7 reduce-scatter.1
where the time goes:
time: 682 us; the launch traced here: 678 us
  blocking collectives  444 us (65%)
  matrix products  106 us (16%)
  waiting for transfers between devices  85.2 us (12%)
  between operations  14.3 us (2%)
  starting transfers between devices  11.1 us (2%)
  other arithmetic  10.7 us (2%)
    pmax x3, blocking collectives, column_lse(): highest = lax.pmax(peaks, 'row')  170 us
    psum x3, blocking collectives, column_lse(): summed = lax.psum(totals * jnp.exp(peaks - highest), 'row')  167 us
    all_to_all x1, blocking collectives, shards(): lax.all_to_all(source_map, 'cluster', split_axis=0, concat_axis=0, tiled=...  94.9 us
    dot_general x56, matrix products, cost_panel(): jnp.einsum('id,jd->ij', source_rows, target_rows, preferred_element_type=...  79.3 us
    all_gather x1, waiting for transfers between devices, shards(): cluster_targets = lax.all_gather(local_targets, 'row', axis=0, tiled=True)  39.4 us
    reduce_scatter x1, waiting for transfers between devices, shards(): lax.psum_scatter(jnp.einsum('ij,id->jd', weights, local_sources, preferre...  33.8 us
    dot_general x8, matrix products, accumulate(): jnp.dot(weights, block, preferred_element_type=jnp.float32)  15 us
  transfers between devices with their start and end apart: 4, of which 4 were waited for; matrix products, arithmetic and copies ran while one was open for 5% of the time, Pallas kernels for 0%

commit v1 on v0

--- a/solution.py
+++ b/solution.py
@@ -1,3 +1,4 @@
+import functools
 import math
 import jax
 import jax.numpy as jnp
@@ -6,6 +7,14 @@
 
 ITERS = 3
 entropy_weight = 0.02
+
+
+def records_choose(chunk, axis_tag):
+    d_next = jax.lax.all_gather(chunk, axis_tag)
+    return jnp.sum(d_next, 0)
+
+
+unite_block = functools.partial(records_choose, axis_tag="row")
 
 
 def square_sums(matrix):
@@ -85,7 +94,7 @@
         peaks = peaks.reshape(-1)
         totals = totals.reshape(-1)
         highest = lax.pmax(peaks, "row")
-        summed = lax.psum(totals * jnp.exp(peaks - highest), "row")
+        summed = unite_block(totals * jnp.exp(peaks - highest))
         return highest + jnp.log(summed)
 
     target_potential = jnp.zeros((columns,), jnp.float32)

time: 682 us -> 544 us (0.80)
  blocking collectives: 444 us -> 302 us
    psum x3 -> x0, blocking collectives: 167 us -> none  [column_lse(): summed = lax.psum(totals * jnp.exp(peaks - highest), 'row')]
    all_gather x0 -> x3, blocking collectives: none -> 48.4 us  [records_choose(): d_next = jax.lax.all_gather(chunk, axis_tag)]
    all_to_all x1, blocking collectives: 94.9 us -> 67.9 us  [shards(): lax.all_to_all(source_map, 'cluster', split_axis=0, concat_axis=0, tiled=...]
  transfers between devices with their start and end apart: 4 -> 4, of which waited for: 4 -> 4; matrix products, arithmetic and copies ran while one was open for 5% -> 6% of each run, Pallas kernels for 0% -> 0%
where the time goes in v1:
time: 544 us; the launch traced here: 541 us
  blocking collectives  302 us (56%)
  matrix products  108 us (20%)
  waiting for transfers between devices  86.3 us (16%)
  between operations  14.4 us (3%)
  starting transfers between devices  11.1 us (2%)
  other arithmetic  10.9 us (2%)
    pmax x3, blocking collectives, column_lse(): highest = lax.pmax(peaks, 'row')  174 us
    dot_general x56, matrix products, cost_panel(): jnp.einsum('id,jd->ij', source_rows, target_rows, preferred_element_type=...  79.3 us
    all_to_all x1, blocking collectives, shards(): lax.all_to_all(source_map, 'cluster', split_axis=0, concat_axis=0, tiled=...  67.9 us
    all_gather x3, blocking collectives, records_choose(): d_next = jax.lax.all_gather(chunk, axis_tag)  48.4 us
    all_gather x1, waiting for transfers between devices, shards(): cluster_targets = lax.all_gather(local_targets, 'row', axis=0, tiled=True)  39.4 us
    reduce_scatter x1, waiting for transfers between devices, shards(): lax.psum_scatter(jnp.einsum('ij,id->jd', weights, local_sources, preferre...  35 us
    dot_general x8, matrix products, accumulate(): jnp.dot(weights, block, preferred_element_type=jnp.float32)  17.3 us
    all_to_all x1, blocking collectives, shards(): lax.all_to_all(sent_targets, 'cluster', split_axis=0, concat_axis=0, tile...  12.2 us
  transfers between devices with their start and end apart: 4, of which 4 were waited for; matrix products, arithmetic and copies ran while one was open for 6% of the time, Pallas kernels for 0%

profile of v1, /device:TPU:1, one launch (start us, length us, event | category | flops | bytes accessed | tf_op | source)
XLA Modules:
  0.0 540.7 jit_solution(14654441921452973470)
XLA Ops:
  9.0 12.2 %all_to_all.48 = bf16[8,32,512]{2,1,0:T(8,128)(2,1)} all-to-all(bf16[8,32,512]{2,1,0:T(8,128)(2,1)S(1)} %bitcast.260), channel_id=1, replica_groups=mesh['cluster'=8,'row'=16] {'cluster'}, dimensions={0} | all-to-all | bytes 524288 | tf_op jit(solution)/shard_map/all_to_all | solution.py:49
  21.2 1.9 convolution_convert_fusion.4
  23.1 4.4 all-to-all-start
  27.6 6.4 %all-to-all-done = bf16[8,32,512]{2,1,0:T(8,128)(2,1)S(1)} async-done(((bf16[8,32,512]{2,1,0:T(8,128)(2,1)}), bf16[8,32,512]{2,1,0:T(8,128)(2,1)S(1)}, u32[]{:S(2)}, u32[]{:S(2)}) %all-to-all-start) | async-done | bytes 262176 | tf_op jit(solution)/shard_map/all_to_all | solution.py:48
  34.2 39.4 %all-gather.5.cloned.1.call-done = bf16[4096,512]{1,0:T(8,128)(2,1)} async-done(((bf16[256,512]{1,0:T(8,128)(2,1)}), bf16[4096,512]{1,0:T(8,128)(2,1)}) %all-gather.5.cloned.1.call-update) | async-done | bytes 4194320 | tf_op jit(solution)/shard_map/all_gather | solution.py:51
  73.6 3.1 multiply_reduce_fusion
  76.7 12.7 %while.102 = (s32[]{:T(128)}, f32[256]{0:T(256)S(1)}, f32[256]{0:T(256)S(1)}, f32[256]{0:T(256)S(1)}, f32[8,512]{1,0:T(8,128)S(1)}, /*index=5*/bf16[8,512,512]{2...) while((s32[]{:T(128)}, f32[256]{0:T(256)S(1)}, f32[256]{0:T(256)S(1)}, ...), condition=%wide.region_5.6_spmd.clone, body=%wide.region_2.5_spmd.clone.sunk | while | flops 135398656 | bytes 1856108 | solution.py:77
  89.5 13.7 %while.99 = (s32[]{:T(128)}, f32[8,512]{1,0:T(8,128)S(1)}, f32[8,512]{1,0:T(8,128)S(1)}, f32[256]{0:T(256)S(1)}, f32[256]{0:T(256)S(1)}, /*index=5*/f32[8,512]{1...) while((s32[]{:T(128)}, f32[8,512]{1,0:T(8,128)S(1)}, ...), condition=%wide.region_9.10_spmd, body=%wide.region_6.9_spmd.sunk | while | flops 135396352 | bytes 1858161 | solution.py:93
  89.5 1.4 fusion.151
  91.2 1.4 fusion.151
  92.9 1.4 fusion.151
  94.6 1.4 fusion.151
  96.4 1.4 fusion.151
  98.1 1.4 fusion.151
  99.8 1.4 fusion.151
  101.5 1.4 fusion.151
  103.2 58.3 %pmax.21 = f32[4096]{0:T(1024)S(1)} all-reduce(f32[4096]{0:T(1024)S(1)} %bitcast.268), channel_id=1, replica_groups=mesh['cluster'=8,'row'=16] {'row'}, use_global_device_ids=true, to_apply=%region_10.11 | all-reduce | flops 4096 | bytes 32768 | tf_op jit(solution)/shard_map/pmax | solution.py:96
  161.5 16.0 %all-gather = f32[65536]{0:T(1024)S(1)} all-gather(f32[4096]{0:T(1024)S(1)} %exponential_multiply_fusion.2), channel_id=2, replica_groups=mesh['cluster'=8,'row'=16] {'row'}, dimensions={0}, use_global_device_ids=true | all-gather | bytes 278528 | tf_op jit(solution)/shard_map/all_gather | solution.py:13
  177.7 12.8 %while.103 = (s32[]{:T(128)}, f32[256]{0:T(256)S(1)}, f32[256]{0:T(256)S(1)}, f32[8,512]{1,0:T(8,128)S(1)}, f32[256]{0:T(256)S(1)}, /*index=5*/f32[8,512]{1,0:T(...) while((s32[]{:T(128)}, f32[256]{0:T(256)S(1)}, ...), condition=%wide.region_15.16_spmd.clone, body=%wide.region_12.15_spmd.clone.sunk | while | flops 135398656 | bytes 1862260 | solution.py:77
  182.5 1.4 fusion.161
  188.9 1.4 fusion.161
  190.5 13.7 %while.100 = (s32[]{:T(128)}, f32[8,512]{1,0:T(8,128)S(1)}, f32[8,512]{1,0:T(8,128)S(1)}, f32[256]{0:T(256)S(1)}, f32[256]{0:T(256)S(1)}, /*index=5*/f32[8,512]{...) while((s32[]{:T(128)}, f32[8,512]{1,0:T(8,128)S(1)}, ...), condition=%wide.region_19.20_spmd, body=%wide.region_16.19_spmd.sunk | while | flops 135396352 | bytes 1858161 | solution.py:93
  190.6 1.4 fusion.153
  192.3 1.4 fusion.153
  194.0 1.4 fusion.153
  195.7 1.4 fusion.153
  197.4 1.4 fusion.153
  199.1 1.4 fusion.153
  200.9 1.4 fusion.153
  202.6 1.4 fusion.153
  204.3 58.1 %pmax.22 = f32[4096]{0:T(1024)S(1)} all-reduce(f32[4096]{0:T(1024)S(1)} %bitcast.270), channel_id=1, replica_groups=mesh['cluster'=8,'row'=16] {'row'}, use_global_device_ids=true, to_apply=%region_20.21 | all-reduce | flops 4096 | bytes 32768 | tf_op jit(solution)/shard_map/pmax | solution.py:96
  262.4 16.6 %all-gather.1 = f32[65536]{0:T(1024)S(1)} all-gather(f32[4096]{0:T(1024)S(1)} %exponential_multiply_fusion.1), channel_id=3, replica_groups=mesh['cluster'=8,'row'=16] {'row'}, dimensions={0}, use_global_device_ids=true | all-gather | bytes 278528 | tf_op jit(solution)/shard_map/all_gather | solution.py:13
  279.2 12.8 %while.104 = (s32[]{:T(128)}, f32[256]{0:T(256)S(1)}, f32[256]{0:T(256)S(1)}, f32[8,512]{1,0:T(8,128)S(1)}, f32[256]{0:T(256)S(1)}, /*index=5*/f32[8,512]{1,0:T(...) while((s32[]{:T(128)}, f32[256]{0:T(256)S(1)}, ...), condition=%wide.region_25.26_spmd.clone, body=%wide.region_22.25_spmd.clone.sunk | while | flops 135398656 | bytes 1862260 | solution.py:77
  279.2 1.4 fusion.165
  285.6 1.4 fusion.165
  292.0 13.7 %while.101 = (s32[]{:T(128)}, f32[8,512]{1,0:T(8,128)S(1)}, f32[8,512]{1,0:T(8,128)S(1)}, f32[256]{0:T(256)S(1)}, f32[256]{0:T(256)S(1)}, /*index=5*/f32[8,512]{...) while((s32[]{:T(128)}, f32[8,512]{1,0:T(8,128)S(1)}, ...), condition=%wide.region_29.30_spmd, body=%wide.region_26.29_spmd.sunk | while | flops 135396352 | bytes 1858161 | solution.py:93
  292.1 1.4 fusion.155
  293.8 1.4 fusion.155
  295.5 1.4 fusion.155
  297.2 1.4 fusion.155
  298.9 1.4 fusion.155
  300.7 1.4 fusion.155
  302.4 1.4 fusion.155
  304.1 1.4 fusion.155
  305.8 57.6 %pmax.23 = f32[4096]{0:T(1024)S(1)} all-reduce(f32[4096]{0:T(1024)S(1)} %bitcast.272), channel_id=1, replica_groups=mesh['cluster'=8,'row'=16] {'row'}, use_global_device_ids=true, to_apply=%region_30.31 | all-reduce | flops 4096 | bytes 32768 | tf_op jit(solution)/shard_map/pmax | solution.py:96
  363.4 15.8 %all-gather.2 = f32[65536]{0:T(1024)S(1)} all-gather(f32[4096]{0:T(1024)S(1)} %exponential_multiply_fusion), channel_id=4, replica_groups=mesh['cluster'=8,'row'=16] {'row'}, dimensions={0}, use_global_device_ids=true | all-gather | bytes 278528 | tf_op jit(solution)/shard_map/all_gather | solution.py:13
  379.3 7.0 %convolution_convert_fusion = bf16[4096,512]{1,0:T(8,128)(2,1)} fusion(bf16[256,512]{1,0:T(8,128)(2,1)S(1)} %get-tuple-element.1322, bf16[4096,512]{1,0:T(8,128)(2,1)} %bitcast.254, f32[4096]{0:T(1024)S(1)} %get-tuple-element.614, f32[4096]{0:T(1024)S(1)} %multiply_reduce_fusion, f32[256]{0:T(256)S(1)} %get-tuple-element.1343, f32[256]{0:T(256)S(1)} %get-tuple-element.1345), kind=kOutput, calls=%fused_computation.123 | convolution fusion | flops 2157969408 | bytes 8685568 | tf_op jit(solution)/shard_map/ij,id->jd/dot_general | solution.py:112
  386.3 12.8 %while.105 = (s32[]{:T(128)}, f32[256]{0:T(256)S(1)}, f32[256]{0:T(256)S(1)}, f32[8,512]{1,0:T(8,128)S(1)}, f32[256]{0:T(256)S(1)}, /*index=5*/f32[8,512]{1,0:T(...) while((s32[]{:T(128)}, f32[256]{0:T(256)S(1)}, ...), condition=%wide.region_35.36_spmd.clone, body=%wide.region_32.35_spmd.clone.sunk | while | flops 135398656 | bytes 1862260 | solution.py:77
  388.0 1.4 fusion.169
  389.6 1.4 fusion.169
  396.0 1.4 fusion.169
  399.2 17.6 %while.106 = (s32[]{:T(128)}, f32[256,512]{1,0:T(8,128)S(1)}, f32[8,512]{1,0:T(8,128)S(1)}, f32[256]{0:T(256)S(1)}, f32[8,512]{1,0:T(8,128)S(1)}, /*index=5*/bf1...) while((s32[]{:T(128)}, f32[256,512]{1,0:T(8,128)S(1)}, ...), condition=%wide.region_37.38_spmd.clone, body=%wide.region_36.37_spmd.clone.sunk | while | flops 269746176 | bytes 2374771 | solution.py:129
  399.2 2.1 convolution_add_fusion.2
  401.4 2.1 convolution_add_fusion.2
  403.6 2.1 convolution_add_fusion.2
  405.8 2.2 convolution_add_fusion.2
  408.0 2.1 convolution_add_fusion.2
  410.2 2.2 convolution_add_fusion.2
  412.5 2.1 convolution_add_fusion.2
  414.7 2.1 convolution_add_fusion.2
  416.9 67.9 %all_to_all.49 = bf16[8,32,512]{2,1,0:T(8,128)(2,1)S(1)} all-to-all(bf16[8,32,512]{2,1,0:T(8,128)(2,1)S(1)} %bitcast.255), channel_id=1, replica_groups=mesh['cluster'=8,'row'=16] {'cluster'}, dimensions={0} | all-to-all | bytes 524288 | tf_op jit(solution)/shard_map/all_to_all | solution.py:136
  484.7 35.0 %reduce-scatter.2.cloned.1.call-done = bf16[256,512]{1,0:T(8,128)(2,1)} async-done(((bf16[4096,512]{1,0:T(8,128)(2,1)}), bf16[256,512]{1,0:T(8,128)(2,1)}) %reduce-scatter.2.cloned.1.call-update) | async-done | bytes 262160 | tf_op jit(solution)/shard_map/reduce_scatter | solution.py:111
  519.7 6.7 %all-to-all-start.3 = ((bf16[8,32,512]{2,1,0:T(8,128)(2,1)}), bf16[8,32,512]{2,1,0:T(8,128)(2,1)S(1)}, u32[]{:S(2)}, u32[]{:S(2)}) async-start(bf16[8,32,512]{2,1,0:T(8,128)(2,1)} %bitcast.261), calls=%async_computation.4 | async-start | bytes 524288 | tf_op jit(solution)/shard_map/all_to_all | solution.py:137
  527.4 5.5 %all-to-all-done.3 = bf16[8,32,512]{2,1,0:T(8,128)(2,1)S(1)} async-done(((bf16[8,32,512]{2,1,0:T(8,128)(2,1)}), bf16[8,32,512]{2,1,0:T(8,128)(2,1)S(1)}, u32[]{:S(2)}, u32[]{:S(2)}) %all-to-all-start.3) | async-done | bytes 262176 | tf_op jit(solution)/shard_map/all_to_all | solution.py:137
  (346 shorter events, 50.3 us)
Async XLA Ops:
  7.2 1.0 copy-start
  7.2 66.4 %all-gather.5.cloned.1.call-start = ((), (), s32[]{:S(2)}) async-start(), calls=%async_computation.5 | async-start | bytes 4456448 | tf_op jit(solution)/shard_map/all_gather | solution.py:51
  23.1 10.8 %all-to-all-start = ((bf16[8,32,512]{2,1,0:T(8,128)(2,1)}), bf16[8,32,512]{2,1,0:T(8,128)(2,1)S(1)}, u32[]{:S(2)}, u32[]{:S(2)}) async-start(bf16[8,32,512]{2,1,0:T(8,128)(2,1)} %bitcast.15), calls=%async_computation | async-start | bytes 524288 | tf_op jit(solution)/shard_map/all_to_all | solution.py:48
  27.5 492.2 %reduce-scatter.2.cloned.1.call-start = ((), (), s32[]{:S(2)}) async-start(), calls=%async_computation.6 | async-start | bytes 4456448 | tf_op jit(solution)/shard_map/reduce_scatter | solution.py:111
  399.2 127.2 %copy-start.1 = (s32[256]{0:T(256)S(1)}, s32[256]{0:T(256)}, u32[]{:S(2)}) copy-start(s32[256]{0:T(256)} %param.22) | copy-start | bytes 3076
  399.2 133.7 %copy-start.2 = (s32[256]{0:T(256)S(1)}, s32[256]{0:T(256)}, u32[]{:S(2)}) copy-start(s32[256]{0:T(256)} %param.23) | copy-start | bytes 3076
  519.7 13.2 %all-to-all-start.3 = ((bf16[8,32,512]{2,1,0:T(8,128)(2,1)}), bf16[8,32,512]{2,1,0:T(8,128)(2,1)S(1)}, u32[]{:S(2)}, u32[]{:S(2)}) async-start(bf16[8,32,512]{2,1,0:T(8,128)(2,1)} %bitcast.261), calls=%async_computation.4 | async-start | bytes 524288 | tf_op jit(solution)/shard_map/all_to_all | solution.py:137
Sparse Core Ops, SparseCore 0:
  21.3 52.2 all-gather.4
  386.4 133.2 reduce-scatter.1
